TPU v7x, 32 devices: a whole 2x2x4 slice. The times are simulated.
32 devices in a mesh: slab: 16 (over z, x, core), vec: 2 (over y).
Axes of the slice: x: 2, y: 2, z: 4, core: 2. Of those that a mesh axis runs over, the one named last changes fastest.
Arguments:
- block: bfloat16 [64, 3, 16, 16, 128], P('vec', None, 'slab'), may hold values from -8 to 8
- labels: int32 [16, 16, 128], P('slab'), may hold values from 0 to 3
- flags: int32 [16, 16, 128], P('slab'), may hold values 0 or 1
- stiffness: float32 [4], replicated, may hold values from 0.25 to 2.5
- density: float32 [4], replicated, may hold values from 0.5 to 4
Outputs:
- filtered: bfloat16 [64, 3, 16, 16, 128], P('vec', None, 'slab')
- gram: float32 [64, 64], P('vec')
Inputs may be any that keep to these rules, and one draw needn't show every extreme that they name: `labels`: 0 steel, 1 weld, 2 bearing, 3 void filler.
All inputs are finite; a program needn't handle non-finite values. No bound on the sum of `flags` on one device may be relied on, other than what follows from the above.
Results may differ from a plain program's by a relative error of at most 0.0049.
Values may be sent and summed in bfloat16 or wider, within the bound.
A program may use at most 64 MiB of HBM per device.

v0:
```python
import jax
import jax.numpy as jnp
from jax import lax
from jax.sharding import PartitionSpec as P

axial_modulus = 0.75
shear_modulus = 0.25
dilation_modulus = 0.5


def padded_2(block, sides, width):
    for axis, dim in sides:
        count = lax.axis_size(axis)
        forward = [(i, i + 1) for i in range(count - 1)]
        backward = [(target, source) for source, target in forward]
        low = lax.ppermute(
            lax.slice_in_dim(block, block.shape[dim] - width, None, axis=dim), axis, forward
        )
        high = lax.ppermute(lax.slice_in_dim(block, 0, width, axis=dim), axis, backward)
        block = jnp.concatenate([low, block, high], axis=dim)
    return block


def lookup_table(table, labels):
    summed = jnp.zeros(labels.shape, jnp.float32)
    for material in range(table.shape[0]):
        summed = summed + jnp.where(labels == material, table[material], jnp.float32(0.0))
    return summed


def stencil_pass(values, axis_index, operation):
    length = values.shape[axis_index] - 2
    lower = lax.slice_in_dim(values, 0, length, axis=axis_index)
    middle = lax.slice_in_dim(values, 1, length + 1, axis=axis_index)
    higher = lax.slice_in_dim(values, 2, length + 2, axis=axis_index)
    if operation == "avg":
        return (lower + 4.0 * middle + higher) / 6.0
    if operation == "second":
        return lower - 2.0 * middle + higher
    return (higher - lower) * 0.5


def separable(values, operations):
    for position in range(3):
        values = stencil_pass(values, position + 1, operations[position])
    return values


def navier(padded):
    components = [padded[:, source] for source in range(3)]
    results = []
    for target in range(3):
        summed = 0.0
        for direction in range(3):
            operations = ["avg", "avg", "avg"]
            operations[direction] = "second"
            factor = axial_modulus if direction == target else shear_modulus
            summed = summed - factor * separable(components[target], operations)
        for source in range(3):
            if source != target:
                operations = ["avg", "avg", "avg"]
                operations[target] = "first"
                operations[source] = "first"
                summed = summed - dilation_modulus * separable(components[source], operations)
        results.append(summed)
    return jnp.stack(results, axis=1)


def shards(block, labels, flags, stiffness, density):
    gain = jnp.sqrt(lookup_table(stiffness, labels)) * (1 - flags).astype(jnp.float32)
    mass = lookup_table(density, labels)
    scaled = (gain * block.astype(jnp.float32)).astype(jnp.bfloat16)
    padded = padded_2(scaled, (("slab", 2),), 1)
    padded = jnp.pad(padded.astype(jnp.float32), ((0, 0), (0, 0), (0, 0), (1, 1), (1, 1)))
    summed = navier(padded)
    filtered = (gain * summed).astype(jnp.bfloat16)
    rows_flat = filtered.reshape(
        filtered.shape[0], 3, filtered.shape[2] * filtered.shape[3], filtered.shape[4]
    )
    gathered = lax.all_to_all(rows_flat, "vec", split_axis=2, concat_axis=0, tiled=True)
    vec_count = gathered.shape[0]
    group_count = filtered.shape[0]
    share_rows = gathered.shape[2]
    mass_rows = mass.reshape(-1, mass.shape[2])
    mass_share = lax.dynamic_slice_in_dim(
        mass_rows, lax.axis_index("vec") * share_rows, share_rows, 0
    )
    weighted = (mass_share * gathered.astype(jnp.float32)).astype(jnp.bfloat16)
    partial_gram = lax.dot_general(
        gathered.reshape(vec_count, -1),
        weighted.reshape(vec_count, -1),
        (((1,), (1,)), ((), ())),
        preferred_element_type=jnp.float32,
    )
    unknowns = 3 * filtered.shape[2] * lax.axis_size("slab") * filtered.shape[3] * filtered.shape[4]
    summed_gram = lax.psum(partial_gram, ("slab", "vec"))
    row_block = lax.dynamic_slice_in_dim(
        summed_gram, lax.axis_index("vec") * group_count, group_count, 0
    )
    gram = row_block / jnp.float32(unknowns)
    return (filtered, gram)


def solution(mesh):
    in_specs = (
        P("vec", None, "slab", None, None),
        P("slab", None, None),
        P("slab", None, None),
        P(),
        P(),
    )
    out_specs = (P("vec", None, "slab", None, None), P("vec", None))
    return jax.shard_map(shards, mesh=mesh, in_specs=in_specs, out_specs=out_specs, check_vma=False)
```

profile of v0, /device:TPU:0, one launch (start us, length us, event | category | flops | bytes accessed | tf_op | source)
XLA Modules:
  0.0 80.2 jit_solution(18236181936846677165)
XLA Ops:
  0.6 1.5 %fusion.65 = (f32[1]{0:T(128)}, f32[1]{0:T(128)}, f32[1]{0:T(128)}, f32[1]{0:T(128)}) fusion(f32[4]{0:T(128)} %param.8), kind=kLoop, calls=%fused_computation.140 | loop fusion | bytes 32 | tf_op jit(solution)/shard_map/slice | solution.py:27
  2.1 3.3 %multiply_bitcast_fusion = (f32[16,128]{1,0:T(8,128)S(1)}, pred[1,16,128]{2,1,0:T(8,128)(4,1)S(1)}, pred[1,16,128]{2,1,0:T(8,128)(4,1)S(1)}, pred[1,16,128]{2,1,0:T(8,128)(4,1)S(1)}, pred[1,16,128]{2,1,0:T(8,128)(4,1)S(1)}) fusion(s32[1,16,128]{2,1,0:T(8,128)} %param.7, f32[]{:T(128)} %bitcast.3, f32[]{:T(128)} %bitcast.2, f32[]{:T(128)} %bitcast.1, ...), kind=kLoop, calls=%fused_computation.133 | loop fusion | flops 28672 | bytes 32784 | tf_op jit(solution)/shard_map/mul | solution.py:76
  5.4 1.1 %multiply_convert_fusion.1 = bf16[32,3,1,16,128]{4,0,3,2,1:T(8,128)(2,1)S(1)} fusion(bf16[32,3,1,16,128]{4,3,2,1,0:T(8,128)(2,1)} %param.5, f32[16,128]{1,0:T(8,128)S(1)} %get-tuple-element.4), kind=kLoop, calls=%fused_computation.21 | loop fusion | flops 589824 | bytes 794624 | tf_op jit(solution)/shard_map/convert_element_type | solution.py:72
  6.5 1.3 %collective-permute-start.1 = (bf16[32,3,1,16,128]{4,0,3,2,1:T(8,128)(2,1)S(1)}, bf16[32,3,1,16,128]{4,0,3,2,1:T(8,128)(2,1)S(1)}, u32[]{:S(2)}, u32[]{:S(2)}) collective-permute-start(bf16[32,3,1,16,128]{4,0,3,2,1:T(8,128)(2,1)S(1)} %multiply_convert_fusion.1), channel_id=1, source_target_pairs={{2,0},{4,2},{6,4},{8,6},{10,8},{12,10},{14,12},{16,14},{18,16},{20... | collective-permute-start | bytes 1179656 | tf_op jit(solution)/shard_map/ppermute | solution.py:19
  7.8 3.1 %collective-permute-start = (bf16[32,3,1,16,128]{4,0,3,2,1:T(8,128)(2,1)S(1)}, bf16[32,3,1,16,128]{4,0,3,2,1:T(8,128)(2,1)S(1)}, u32[]{:S(2)}, u32[]{:S(2)}) collective-permute-start(bf16[32,3,1,16,128]{4,0,3,2,1:T(8,128)(2,1)S(1)} %multiply_convert_fusion.1), channel_id=1, source_target_pairs={{0,2},{2,4},{4,6},{6,8},{8,10},{10,12},{12,14},{14,16},{16,18},{18... | collective-permute-start | bytes 1179656 | tf_op jit(solution)/shard_map/ppermute | solution.py:16
  10.8 1.5 %fusion.64 = (f32[1]{0:T(128)}, f32[1]{0:T(128)}, f32[1]{0:T(128)}, f32[1]{0:T(128)}) fusion(f32[4]{0:T(128)} %param.9), kind=kLoop, calls=%fused_computation.139 | loop fusion | bytes 32 | tf_op jit(solution)/shard_map/slice | solution.py:27
  12.3 2.6 %add_bitcast_fusion = f32[8,128]{1,0:T(8,128)S(1)} fusion(pred[1,16,128]{2,1,0:T(8,128)(4,1)S(1)} %get-tuple-element.8, s32[]{:T(128)S(6)} %select_n.39, pred[1,16,128]{2,1,0:T(8,128)(4,1)S(1)} %get-tuple-element.7, pred[1,16,128]{2,1,0:T(8,128)(4,1)S(1)} %get-tuple-element.6, pred[1,16,128]{2,1,0:T(8,128)(4,1)S(1)} %get-tuple-element.5, f32[]{:T(128)} %bitcast.20, ...), kind=kLoop, calls=%fused_computation.134 | loop fusion | flops 7168 | bytes 8212 | tf_op jit(solution)/shard_map/mul | solution.py:88
  14.9 0.0 collective-permute-done.1
  14.9 0.0 collective-permute-done
  14.9 1.7 %fusion.3 = f32[32,3,3,18,130]{4,0,3,2,1:T(8,128)S(1)} fusion(bf16[32,3,1,16,128]{4,0,3,2,1:T(8,128)(2,1)S(1)} %collective-permute-done.1, bf16[32,3,1,16,128]{4,0,3,2,1:T(8,128)(2,1)S(1)} %multiply_convert_fusion.1, bf16[32,3,1,16,128]{4,0,3,2,1:T(8,128)(2,1)S(1)} %collective-permute-done), kind=kLoop, calls=%fused_computation.8 | loop fusion | flops 12804480 | bytes 3875328 | tf_op jit(solution)/shard_map/jit(_pad)/pad | solution.py:74
  16.6 0.9 %slice_bitcast_fusion = (f32[32,3,18,130]{3,0,2,1:T(8,128)S(1)}, f32[32,3,18,130]{3,0,2,1:T(8,128)S(1)}, f32[32,3,18,130]{3,0,2,1:T(8,128)S(1)}) fusion(f32[32,3,3,18,130]{4,0,3,2,1:T(8,128)S(1)} %fusion.3), kind=kLoop, calls=%fused_computation.13 | loop fusion | bytes 5391360 | tf_op jit(solution)/shard_map/squeeze | solution.py:50
  17.4 0.5 subtract_multiply_fusion.1
  17.9 0.1 fusion.16
  18.0 0.1 fusion.12
  18.1 0.1 fusion.14
  18.3 0.2 subtract_multiply_fusion.4
  18.5 0.2 subtract_add_fusion.4
  18.7 0.3 subtract_add_fusion.2
  19.0 0.1 subtract_add_fusion.5
  19.2 0.2 subtract_multiply_fusion.5
  19.3 0.6 fusion.23
  20.0 0.7 fusion.37
  20.6 0.7 fusion.51
  21.3 0.8 %fusion.8 = bf16[32,3,16,128]{3,0,1,2:T(8,128)(2,1)} fusion(f32[32,1,16,128]{3,0,1,2:T(8,128)S(1)} %fusion.23, f32[32,1,16,128]{3,0,1,2:T(8,128)S(1)} %bitcast.46, f32[32,1,16,128]{3,0,1,2:T(8,128)S(1)} %bitcast.48, f32[16,128]{1,0:T(8,128)S(1)} %get-tuple-element.4), kind=kLoop, calls=%fused_computation.19 | loop fusion | flops 786432 | bytes 1187840 | tf_op jit(solution)/shard_map/convert_element_type | solution.py:76
  22.2 4.2 %all-to-all-start = ((bf16[32,3,16,128]{3,0,1,2:T(8,128)(2,1)}), bf16[32,3,16,128]{3,0,1,2:T(8,128)(2,1)S(1)}, u32[]{:S(2)}, u32[]{:S(2)}) async-start(bf16[32,3,16,128]{3,0,1,2:T(8,128)(2,1)} %fusion.8), calls=%async_computation | async-start | bytes 786432 | tf_op jit(solution)/shard_map/all_to_all | solution.py:80
  26.4 0.1 fusion.7
  26.5 0.9 %copy.22 = bf16[32,3,1,16,128]{4,3,2,1,0:T(8,128)(2,1)} copy(bf16[32,3,1,16,128]{4,0,3,2,1:T(8,128)(2,1)S(1)} %fusion.7) | data formatting | bytes 786432
  27.4 5.1 %all-to-all-done = bf16[32,3,16,128]{3,0,1,2:T(8,128)(2,1)S(1)} async-done(((bf16[32,3,16,128]{3,0,1,2:T(8,128)(2,1)}), bf16[32,3,16,128]{3,0,1,2:T(8,128)(2,1)S(1)}, u32[]{:S(2)}, u32[]{:S(2)}) %all-to-all-start) | async-done | bytes 393248 | tf_op jit(solution)/shard_map/all_to_all | solution.py:80
  32.5 0.2 copy.27
  32.6 0.2 multiply_convert_fusion
  32.8 0.2 reshape.87
  33.0 0.2 convert_element_type.45
  33.1 0.3 fusion.66
  33.4 46.2 %psum.7 = f32[64,64]{1,0:T(8,128)S(1)} all-reduce(f32[64,64]{1,0:T(8,128)S(1)} %fusion.66), channel_id=1, replica_groups=mesh['slab'=16,'vec'=2] {'slab','vec'}, use_global_device_ids=true, to_apply=%region_0.1 | all-reduce | flops 4096 | bytes 32768 | tf_op jit(solution)/shard_map/psum | solution.py:96
  79.6 0.6 dynamic-slice_multiply_fusion
  (1 shorter events, 0.0 us)
Async XLA Ops:
  6.5 8.4 %collective-permute-start.1 = (bf16[32,3,1,16,128]{4,0,3,2,1:T(8,128)(2,1)S(1)}, bf16[32,3,1,16,128]{4,0,3,2,1:T(8,128)(2,1)S(1)}, u32[]{:S(2)}, u32[]{:S(2)}) collective-permute-start(bf16[32,3,1,16,128]{4,0,3,2,1:T(8,128)(2,1)S(1)} %multiply_convert_fusion.1), channel_id=1, source_target_pairs={{2,0},{4,2},{6,4},{8,6},{10,8},{12,10},{14,12},{16,14},{18,16},{20... | collective-permute-start | bytes 1179656 | tf_op jit(solution)/shard_map/ppermute | solution.py:19
  7.8 7.1 %collective-permute-start = (bf16[32,3,1,16,128]{4,0,3,2,1:T(8,128)(2,1)S(1)}, bf16[32,3,1,16,128]{4,0,3,2,1:T(8,128)(2,1)S(1)}, u32[]{:S(2)}, u32[]{:S(2)}) collective-permute-start(bf16[32,3,1,16,128]{4,0,3,2,1:T(8,128)(2,1)S(1)} %multiply_convert_fusion.1), channel_id=1, source_target_pairs={{0,2},{2,4},{4,6},{6,8},{8,10},{10,12},{12,14},{14,16},{16,18},{18... | collective-permute-start | bytes 1179656 | tf_op jit(solution)/shard_map/ppermute | solution.py:16
  22.2 10.3 %all-to-all-start = ((bf16[32,3,16,128]{3,0,1,2:T(8,128)(2,1)}), bf16[32,3,16,128]{3,0,1,2:T(8,128)(2,1)S(1)}, u32[]{:S(2)}, u32[]{:S(2)}) async-start(bf16[32,3,16,128]{3,0,1,2:T(8,128)(2,1)} %fusion.8), calls=%async_computation | async-start | bytes 786432 | tf_op jit(solution)/shard_map/all_to_all | solution.py:80
where the time goes:
time: 80.7 us; the launch traced here: 80.2 us
  blocking collectives  46.2 us (57%)
  other arithmetic  14.1 us (17%)
  starting transfers between devices  8.58 us (11%)
  local copies, waits for them, and re-layouts  5.18 us (6%)
  waiting for transfers between devices  5.07 us (6%)
  between operations  0.83 us (1%)
    psum x1, blocking collectives, shards(): summed_gram = lax.psum(partial_gram, ('slab', 'vec'))  46.2 us
    all_to_all x1, waiting for transfers between devices, shards(): lax.all_to_all(rows_flat, 'vec', split_axis=2, concat_axis=0, tiled=True)  5.06 us
    all_to_all x1, starting transfers between devices, shards(): lax.all_to_all(rows_flat, 'vec', split_axis=2, concat_axis=0, tiled=True)  4.23 us
    mul x1, other arithmetic, shards(): filtered = (gain * summed).astype(jnp.bfloat16)  3.28 us
    ppermute x1, starting transfers between devices, padded_2(): lax.ppermute(lax.slice_in_dim(block, block.shape[dim] - width, None, axis...  3.05 us
    slice x2, local copies, waits for them, and re-layouts, lookup_table(): table[material]  2.92 us
    mul x1, other arithmetic, shards(): weighted = (mass_share * gathered.astype(jnp.float32)).astype(jnp.bfloat16)  2.56 us
    sub x3, other arithmetic, navier(): summed - dilation_modulus * separable(components[source], operations)  1.99 us
  transfers between devices with their start and end apart: 3, of which 1 were waited for; matrix products, arithmetic and copies ran while one was open for 6% of the time, Pallas kernels for 0%

commit v1 on v0

--- a/solution.py
+++ b/solution.py
@@ -93,7 +93,8 @@
         preferred_element_type=jnp.float32,
     )
     unknowns = 3 * filtered.shape[2] * lax.axis_size("slab") * filtered.shape[3] * filtered.shape[4]
-    summed_gram = lax.psum(partial_gram, ("slab", "vec"))
+    terms = lax.all_gather(partial_gram, ("slab", "vec"), axis=0, tiled=False)
+    summed_gram = terms.sum(axis=0)
     row_block = lax.dynamic_slice_in_dim(
         summed_gram, lax.axis_index("vec") * group_count, group_count, 0
     )

time: 80.7 us -> 107 us (1.33)
  blocking collectives: 46.2 us -> 72.7 us
    all_gather x0 -> x1, blocking collectives: none -> 72.7 us  [shards(): terms = lax.all_gather(partial_gram, ('slab', 'vec'), axis=0, tiled=False)]
    psum x1 -> x0, blocking collectives: 46.2 us -> none  [shards(): summed_gram = lax.psum(partial_gram, ('slab', 'vec'))]
  transfers between devices with their start and end apart: 3 -> 3, of which waited for: 1 -> 1; matrix products, arithmetic and copies ran while one was open for 6% -> 5% of each run, Pallas kernels for 0% -> 0%
where the time goes in v1:
time: 107 us
  blocking collectives  72.7 us (68%)
  other arithmetic  14.2 us (13%)
  starting transfers between devices  8.58 us (8%)
  local copies, waits for them, and re-layouts  5.18 us (5%)
  waiting for transfers between devices  5.07 us (5%)
    all_gather x1, blocking collectives, shards(): terms = lax.all_gather(partial_gram, ('slab', 'vec'), axis=0, tiled=False)  72.7 us
    all_to_all x1, waiting for transfers between devices, shards(): lax.all_to_all(rows_flat, 'vec', split_axis=2, concat_axis=0, tiled=True)  5.06 us
    all_to_all x1, starting transfers between devices, shards(): lax.all_to_all(rows_flat, 'vec', split_axis=2, concat_axis=0, tiled=True)  4.23 us
    mul x1, other arithmetic, shards(): filtered = (gain * summed).astype(jnp.bfloat16)  3.28 us
    ppermute x1, starting transfers between devices, padded_2(): lax.ppermute(lax.slice_in_dim(block, block.shape[dim] - width, None, axis...  3.05 us
    slice x2, local copies, waits for them, and re-layouts, lookup_table(): table[material]  2.92 us
    mul x1, other arithmetic, shards(): weighted = (mass_share * gathered.astype(jnp.float32)).astype(jnp.bfloat16)  2.56 us
  transfers between devices with their start and end apart: 3, of which 1 were waited for; matrix products, arithmetic and copies ran while one was open for 5% of the time, Pallas kernels for 0%

profile of v1, /device:TPU:0, one launch (start us, length us, event | category | flops | bytes accessed | tf_op | source)
XLA Modules:
  0.0 106.8 jit_solution(3243046079019689320)
XLA Ops:
  0.6 1.5 %fusion.65 = (f32[1]{0:T(128)}, f32[1]{0:T(128)}, f32[1]{0:T(128)}, f32[1]{0:T(128)}) fusion(f32[4]{0:T(128)} %param.8), kind=kLoop, calls=%fused_computation.140 | loop fusion | bytes 32 | tf_op jit(solution)/shard_map/slice | solution.py:27
  2.1 3.3 %multiply_bitcast_fusion = (f32[16,128]{1,0:T(8,128)S(1)}, pred[1,16,128]{2,1,0:T(8,128)(4,1)S(1)}, pred[1,16,128]{2,1,0:T(8,128)(4,1)S(1)}, pred[1,16,128]{2,1,0:T(8,128)(4,1)S(1)}, pred[1,16,128]{2,1,0:T(8,128)(4,1)S(1)}) fusion(s32[1,16,128]{2,1,0:T(8,128)} %param.7, f32[]{:T(128)} %bitcast.3, f32[]{:T(128)} %bitcast.2, f32[]{:T(128)} %bitcast.1, ...), kind=kLoop, calls=%fused_computation.133 | loop fusion | flops 28672 | bytes 32784 | tf_op jit(solution)/shard_map/mul | solution.py:76
  5.4 1.1 %multiply_convert_fusion.1 = bf16[32,3,1,16,128]{4,0,3,2,1:T(8,128)(2,1)S(1)} fusion(bf16[32,3,1,16,128]{4,3,2,1,0:T(8,128)(2,1)} %param.5, f32[16,128]{1,0:T(8,128)S(1)} %get-tuple-element.4), kind=kLoop, calls=%fused_computation.21 | loop fusion | flops 589824 | bytes 794624 | tf_op jit(solution)/shard_map/convert_element_type | solution.py:72
  6.5 1.3 %collective-permute-start.1 = (bf16[32,3,1,16,128]{4,0,3,2,1:T(8,128)(2,1)S(1)}, bf16[32,3,1,16,128]{4,0,3,2,1:T(8,128)(2,1)S(1)}, u32[]{:S(2)}, u32[]{:S(2)}) collective-permute-start(bf16[32,3,1,16,128]{4,0,3,2,1:T(8,128)(2,1)S(1)} %multiply_convert_fusion.1), channel_id=1, source_target_pairs={{2,0},{4,2},{6,4},{8,6},{10,8},{12,10},{14,12},{16,14},{18,16},{20... | collective-permute-start | bytes 1179656 | tf_op jit(solution)/shard_map/ppermute | solution.py:19
  7.8 3.1 %collective-permute-start = (bf16[32,3,1,16,128]{4,0,3,2,1:T(8,128)(2,1)S(1)}, bf16[32,3,1,16,128]{4,0,3,2,1:T(8,128)(2,1)S(1)}, u32[]{:S(2)}, u32[]{:S(2)}) collective-permute-start(bf16[32,3,1,16,128]{4,0,3,2,1:T(8,128)(2,1)S(1)} %multiply_convert_fusion.1), channel_id=1, source_target_pairs={{0,2},{2,4},{4,6},{6,8},{8,10},{10,12},{12,14},{14,16},{16,18},{18... | collective-permute-start | bytes 1179656 | tf_op jit(solution)/shard_map/ppermute | solution.py:16
  10.8 1.5 %fusion.64 = (f32[1]{0:T(128)}, f32[1]{0:T(128)}, f32[1]{0:T(128)}, f32[1]{0:T(128)}) fusion(f32[4]{0:T(128)} %param.9), kind=kLoop, calls=%fused_computation.139 | loop fusion | bytes 32 | tf_op jit(solution)/shard_map/slice | solution.py:27
  12.3 2.6 %add_bitcast_fusion = f32[8,128]{1,0:T(8,128)S(1)} fusion(pred[1,16,128]{2,1,0:T(8,128)(4,1)S(1)} %get-tuple-element.8, s32[]{:T(128)S(6)} %select_n.39, pred[1,16,128]{2,1,0:T(8,128)(4,1)S(1)} %get-tuple-element.7, pred[1,16,128]{2,1,0:T(8,128)(4,1)S(1)} %get-tuple-element.6, pred[1,16,128]{2,1,0:T(8,128)(4,1)S(1)} %get-tuple-element.5, f32[]{:T(128)} %bitcast.20, ...), kind=kLoop, calls=%fused_computation.134 | loop fusion | flops 7168 | bytes 8212 | tf_op jit(solution)/shard_map/mul | solution.py:88
  14.9 0.0 collective-permute-done.1
  14.9 0.0 collective-permute-done
  14.9 1.7 %fusion.3 = f32[32,3,3,18,130]{4,0,3,2,1:T(8,128)S(1)} fusion(bf16[32,3,1,16,128]{4,0,3,2,1:T(8,128)(2,1)S(1)} %collective-permute-done.1, bf16[32,3,1,16,128]{4,0,3,2,1:T(8,128)(2,1)S(1)} %multiply_convert_fusion.1, bf16[32,3,1,16,128]{4,0,3,2,1:T(8,128)(2,1)S(1)} %collective-permute-done), kind=kLoop, calls=%fused_computation.8 | loop fusion | flops 12804480 | bytes 3875328 | tf_op jit(solution)/shard_map/jit(_pad)/pad | solution.py:74
  16.6 0.9 slice_bitcast_fusion
  17.4 0.5 subtract_multiply_fusion.1
  17.9 0.1 fusion.16
  18.0 0.1 fusion.12
  18.1 0.1 fusion.14
  18.3 0.2 subtract_multiply_fusion.4
  18.5 0.2 subtract_add_fusion.4
  18.7 0.3 subtract_add_fusion.2
  19.0 0.1 subtract_add_fusion.5
  19.2 0.2 subtract_multiply_fusion.5
  19.3 0.6 fusion.23
  20.0 0.7 fusion.37
  20.6 0.7 fusion.51
  21.3 0.8 fusion.8
  22.2 4.2 %all-to-all-start = ((bf16[32,3,16,128]{3,0,1,2:T(8,128)(2,1)}), bf16[32,3,16,128]{3,0,1,2:T(8,128)(2,1)S(1)}, u32[]{:S(2)}, u32[]{:S(2)}) async-start(bf16[32,3,16,128]{3,0,1,2:T(8,128)(2,1)} %fusion.8), calls=%async_computation | async-start | bytes 786432 | tf_op jit(solution)/shard_map/all_to_all | solution.py:80
  26.4 0.1 fusion.7
  26.5 0.9 copy.22
  27.4 5.1 %all-to-all-done = bf16[32,3,16,128]{3,0,1,2:T(8,128)(2,1)S(1)} async-done(((bf16[32,3,16,128]{3,0,1,2:T(8,128)(2,1)}), bf16[32,3,16,128]{3,0,1,2:T(8,128)(2,1)S(1)}, u32[]{:S(2)}, u32[]{:S(2)}) %all-to-all-start) | async-done | bytes 393248 | tf_op jit(solution)/shard_map/all_to_all | solution.py:80
  32.5 0.2 copy.27
  32.6 0.2 multiply_convert_fusion
  32.8 0.2 reshape.87
  33.0 0.2 convert_element_type.45
  33.1 0.3 fusion.66
  33.4 72.7 %all-gather = f32[2048,64]{1,0:T(8,128)S(1)} all-gather(f32[64,64]{1,0:T(8,128)S(1)} %fusion.66), channel_id=2, replica_groups=mesh['slab'=16,'vec'=2] {'slab','vec'}, dimensions={0}, use_global_device_ids=true | all-gather | bytes 540672 | tf_op jit(solution)/shard_map/all_gather | solution.py:96
  106.1 0.1 reduce_sum.9
  106.2 0.6 dynamic-slice_multiply_fusion
  (1 shorter events, 0.0 us)
Async XLA Ops:
  6.5 8.4 %collective-permute-start.1 = (bf16[32,3,1,16,128]{4,0,3,2,1:T(8,128)(2,1)S(1)}, bf16[32,3,1,16,128]{4,0,3,2,1:T(8,128)(2,1)S(1)}, u32[]{:S(2)}, u32[]{:S(2)}) collective-permute-start(bf16[32,3,1,16,128]{4,0,3,2,1:T(8,128)(2,1)S(1)} %multiply_convert_fusion.1), channel_id=1, source_target_pairs={{2,0},{4,2},{6,4},{8,6},{10,8},{12,10},{14,12},{16,14},{18,16},{20... | collective-permute-start | bytes 1179656 | tf_op jit(solution)/shard_map/ppermute | solution.py:19
  7.8 7.1 %collective-permute-start = (bf16[32,3,1,16,128]{4,0,3,2,1:T(8,128)(2,1)S(1)}, bf16[32,3,1,16,128]{4,0,3,2,1:T(8,128)(2,1)S(1)}, u32[]{:S(2)}, u32[]{:S(2)}) collective-permute-start(bf16[32,3,1,16,128]{4,0,3,2,1:T(8,128)(2,1)S(1)} %multiply_convert_fusion.1), channel_id=1, source_target_pairs={{0,2},{2,4},{4,6},{6,8},{8,10},{10,12},{12,14},{14,16},{16,18},{18... | collective-permute-start | bytes 1179656 | tf_op jit(solution)/shard_map/ppermute | solution.py:16
  22.2 10.3 %all-to-all-start = ((bf16[32,3,16,128]{3,0,1,2:T(8,128)(2,1)}), bf16[32,3,16,128]{3,0,1,2:T(8,128)(2,1)S(1)}, u32[]{:S(2)}, u32[]{:S(2)}) async-start(bf16[32,3,16,128]{3,0,1,2:T(8,128)(2,1)} %fusion.8), calls=%async_computation | async-start | bytes 786432 | tf_op jit(solution)/shard_map/all_to_all | solution.py:80
